TPU v7x, 256 devices: a whole 4x4x8 slice. The times are simulated.
256 devices in a mesh: facet: 16 (over x, y), span: 16 (over z, core).
Axes of the slice: x: 4, y: 4, z: 8, core: 2. Of those that a mesh axis runs over, the one named last changes fastest.
Arguments:
- visibilities: bfloat16 [16, 512, 2, 1024], P('span', 'facet'), may hold values from -6 to 6
- coordinates: bfloat16 [16, 512, 2, 1024], P('span', 'facet'), may hold values from 4 to 124
- phases: float32 [16, 512, 1024], P('span', 'facet'), may hold values from -3.140625 to 3.140625
- sub_index: int32 [16, 512], replicated, may hold values from 0 to 4095, as said below
Outputs:
- dirty: float32 [8192, 8192], P(('facet', 'span'))
Inputs may be any that keep to these rules, and one draw needn't show every extreme that they name: `sub_index`: within one span (one row) all 512 subgrid indices differ. A grid block is the set of subgrids with rows f * 4 to (f + 1) * 4 - 1 and columns j * 4 to (j + 1) * 4 - 1 for f < 16, j < 16; at most 4 indices of one row fall in one grid block, and in every row some grid block holds exactly 4 of them.
All inputs are finite; a program needn't handle non-finite values.
Results may differ from a plain program's by a relative error of at most 0.005.
Values may be sent and summed in bfloat16 or wider, within the bound.
No kernel may reach another device: no remote copies, remote signals or barrier semaphores. Data moves between devices by JAX's collectives and lax.ppermute only.
A program may use at most 64 MiB of HBM per device.

v0:
```python
import jax
import jax.numpy as jnp
from jax import lax
from jax.sharding import PartitionSpec as P

N = 8192
P_SIZE = 128
CAP = 4
spread = 0.75


def kernel_rows(positions, cell_index):
    gap_size = cell_index - positions[..., None]
    return jnp.exp(-(gap_size * gap_size) / (2.0 * spread * spread))


def subgrids_of(vis_items, coord_items):
    cell_index = jnp.arange(P_SIZE, dtype=jnp.float32)
    coord_vals = coord_items.astype(jnp.float32)
    row_kernel = kernel_rows(coord_vals[:, 0, :], cell_index)
    col_kernel = kernel_rows(coord_vals[:, 1, :], cell_index).astype(jnp.bfloat16)
    weighted = (vis_items.astype(jnp.float32)[:, :, :, None] * row_kernel[:, None, :, :]).astype(
        jnp.bfloat16
    )
    result = jnp.einsum("ezkp,ekq->ezpq", weighted, col_kernel, preferred_element_type=jnp.float32)
    return result.astype(jnp.bfloat16)


def group_subgrids(group_inputs):
    return subgrids_of(group_inputs[0], group_inputs[1])


def entries(sub_row, target, band_sub, col_sub, span_count):
    side_count = N // P_SIZE
    sub_rows = sub_row // side_count
    sub_cols = sub_row % side_count
    owning_block = sub_rows // band_sub * span_count + sub_cols // col_sub
    local_slot = sub_rows % band_sub * col_sub + sub_cols % col_sub
    inside = (owning_block == target).astype(jnp.int32)
    rank_of = jnp.cumsum(inside) - 1
    picked = (
        (inside[None, :] == 1) & (rank_of[None, :] == jnp.arange(CAP, dtype=jnp.int32)[:, None])
    ).astype(jnp.int32)
    block_num = jnp.arange(sub_row.shape[0], dtype=jnp.int32)
    block_ids = jnp.sum(picked * block_num[None, :], axis=1)
    slot_ids = jnp.sum(picked * local_slot[None, :], axis=1)
    filled = jnp.sum(picked, axis=1) > 0
    return (block_ids, slot_ids, filled)


def phase_table(row_count, col_count, length):
    row_ids = jnp.arange(row_count, dtype=jnp.int32)[:, None]
    col_ids = jnp.arange(col_count, dtype=jnp.int32)[None, :]
    angles = 2.0 * jnp.pi / length * (row_ids * col_ids % length).astype(jnp.float32)
    return (jnp.cos(angles), jnp.sin(angles))


def inverse_dft(real_part, imag_part):
    length = real_part.shape[-1]
    first_len = 64
    second_len = length // first_len
    leading = real_part.shape[:-1]
    split_real = real_part.reshape(leading + (first_len, second_len))
    split_imag = imag_part.reshape(leading + (first_len, second_len))
    highest = lax.Precision.HIGHEST
    cos_first, sin_first = phase_table(first_len, first_len, first_len)
    step_real = jnp.einsum(
        "av,...vb->...ab", cos_first, split_real, precision=highest
    ) - jnp.einsum("av,...vb->...ab", sin_first, split_imag, precision=highest)
    step_imag = jnp.einsum(
        "av,...vb->...ab", cos_first, split_imag, precision=highest
    ) + jnp.einsum("av,...vb->...ab", sin_first, split_real, precision=highest)
    cos_twist, sin_twist = phase_table(first_len, second_len, length)
    twist_real = step_real * cos_twist - step_imag * sin_twist
    twist_imag = step_real * sin_twist + step_imag * cos_twist
    cos_second, sin_second = phase_table(second_len, second_len, second_len)
    out_real = jnp.einsum(
        "...ab,bc->...ac", twist_real, cos_second, precision=highest
    ) - jnp.einsum("...ab,bc->...ac", twist_imag, sin_second, precision=highest)
    out_imag = jnp.einsum(
        "...ab,bc->...ac", twist_real, sin_second, precision=highest
    ) + jnp.einsum("...ab,bc->...ac", twist_imag, cos_second, precision=highest)
    out_real = jnp.swapaxes(out_real, -1, -2).reshape(leading + (length,))
    out_imag = jnp.swapaxes(out_imag, -1, -2).reshape(leading + (length,))
    return (out_real, out_imag)


def shards(visibilities, coordinates, phases, sub_index):
    facet_count = lax.axis_size("facet")
    span_count = lax.axis_size("span")
    side_count = N // P_SIZE
    band_sub = side_count // facet_count
    col_sub = side_count // span_count
    facet_id = lax.axis_index("facet")
    span_id = lax.axis_index("span")
    vis_count = visibilities.shape[3]
    vis_float = visibilities.astype(jnp.float32)
    cosine = jnp.cos(phases)
    sine = jnp.sin(phases)
    real_part = vis_float[:, :, 0, :]
    imag_part = vis_float[:, :, 1, :]
    rotated = jnp.stack(
        [real_part * cosine - imag_part * sine, real_part * sine + imag_part * cosine], axis=2
    ).astype(jnp.bfloat16)
    own_row = lax.dynamic_index_in_dim(sub_index, span_id, 0, keepdims=False)
    targets = facet_id * span_count + jnp.arange(span_count, dtype=jnp.int32)

    def send_table(target):
        return entries(own_row, target, band_sub, col_sub, span_count)

    send_ids, send_slots, send_filled = jax.vmap(send_table)(targets)
    flat_ids = send_ids.reshape(-1)
    flat_filled = send_filled.reshape(-1)
    entry_count = flat_ids.shape[0]
    blank = jnp.zeros((entry_count, 2, vis_count), jnp.bfloat16)
    pieces = (
        lax.all_gather(rotated, "facet", axis=1, tiled=True),
        lax.all_gather(coordinates, "facet", axis=1, tiled=True),
    )
    rows_here = pieces[0].shape[1]
    inside = flat_filled & (flat_ids >= 0) & (flat_ids < rows_here)
    where_row = jnp.clip(flat_ids, 0, rows_here - 1)
    vis_rows = jnp.take(pieces[0][0], where_row, axis=0)
    coord_rows = jnp.take(pieces[1][0], where_row, axis=0)
    keep_mask = inside[:, None, None]
    chosen_vis = jnp.where(keep_mask, vis_rows, blank)
    chosen_coords = jnp.where(keep_mask, coord_rows, blank)
    grouped_vis = chosen_vis.reshape(span_count, CAP, 2, vis_count)
    grouped_coords = chosen_coords.reshape(span_count, CAP, 2, vis_count)
    made_subs = lax.map(group_subgrids, (grouped_vis, grouped_coords))
    arrived = lax.all_to_all(made_subs, "span", split_axis=0, concat_axis=0, tiled=True)
    my_block = facet_id * span_count + span_id

    def recv_table(source_row):
        return entries(source_row, my_block, band_sub, col_sub, span_count)

    recv_ids, recv_slots, recv_filled = jax.vmap(recv_table)(sub_index)
    slots_here = band_sub * col_sub
    slot_range = jnp.arange(slots_here, dtype=jnp.int32)[:, None]
    onehot = (
        (recv_slots.reshape(-1)[None, :] == slot_range) & recv_filled.reshape(-1)[None, :]
    ).astype(jnp.bfloat16)
    items = arrived.reshape(span_count * CAP, 2 * P_SIZE * P_SIZE)
    summed = jnp.dot(onehot, items, preferred_element_type=jnp.float32)
    block = (
        summed.reshape(band_sub, col_sub, 2, P_SIZE, P_SIZE)
        .transpose(2, 0, 3, 1, 4)
        .reshape(2, band_sub * P_SIZE, col_sub * P_SIZE)
    )
    row_block = lax.all_to_all(block, "span", split_axis=1, concat_axis=2, tiled=True)
    half_real, half_imag = inverse_dft(row_block[0], row_block[1])
    half_done = jnp.stack([half_real, half_imag])
    columns = lax.all_to_all(
        lax.all_to_all(half_done, "facet", split_axis=2, concat_axis=1, tiled=True),
        "span",
        split_axis=2,
        concat_axis=1,
        tiled=True,
    )
    row_count = half_done.shape[1]
    col_count = columns.shape[2]
    ordered = (
        columns.reshape(2, span_count, facet_count, row_count, col_count)
        .transpose(0, 4, 2, 1, 3)
        .reshape(2, col_count, N)
    )
    image_real, image_imag = inverse_dft(ordered[0], ordered[1])
    return image_real * (1.0 / N)


def solution(mesh):
    return jax.shard_map(
        shards,
        mesh=mesh,
        in_specs=(
            P("span", "facet", None, None),
            P("span", "facet", None, None),
            P("span", "facet", None),
            P(),
        ),
        out_specs=P(("facet", "span"), None),
        check_vma=False,
    )
```

profile of v0, /device:TPU:1, one launch (start us, length us, event | category | flops | bytes accessed | tf_op | source)
XLA Modules:
  0.0 588.6 jit_solution(86421095488678001)
XLA Ops:
  12.9 49.8 %all-gather.5.cloned.1.call-done = bf16[1,512,2,1024]{3,2,0,1:T(2,128)(2,1)} async-done(((bf16[1,32,2,1024]{3,2,0,1:T(2,128)(2,1)}), bf16[1,512,2,1024]{3,2,0,1:T(2,128)(2,1)}) %all-gather.5.cloned.1.call-update) | async-done | bytes 2097168 | tf_op jit(solution)/shard_map/all_gather | solution.py:118
  65.4 49.1 %all-gather.3.cloned.1.call-done = bf16[1,512,2,1024]{3,2,0,1:T(2,128)(2,1)} async-done(((bf16[1,32,2,1024]{3,2,0,1:T(2,128)(2,1)}), bf16[1,512,2,1024]{3,2,0,1:T(2,128)(2,1)}) %all-gather.3.cloned.1.call-update) | async-done | bytes 2097168 | tf_op jit(solution)/shard_map/all_gather | solution.py:117
  117.9 90.2 %while.10 = (s32[]{:T(128)}, bf16[16,4,2,128,128]{4,3,2,1,0:T(8,128)(2,1)}, bf16[16,4,2,1024]{3,2,1,0:T(2,128)(2,1)S(1)}, bf16[16,4,2,1024]{3,2,1,0:T(2,128)(2,1)S(1)}, s32[]{:T(128)}) while((s32[]{:T(128)}, bf16[16,4,2,128,128]{4,3,2,1,0:T(8,128)(2,1)}, bf16[16,4,2,1024]{3,2,1,0:T(2,128)(2,1)S(1)}, bf16[16,4,2,1024]{3,2,1,0:T(2,128)(2,1)S(1)}, ...), condition=%wide.region_9.11_spmd, body=%wide.region_8.10_spmd.sunk | while | flops 275398656 | bytes 8912977 | solution.py:130
  137.4 3.1 fusion.190
  208.1 8.5 %all-to-all-start = ((bf16[16,4,2,128,128]{4,3,2,1,0:T(8,128)(2,1)}), bf16[16,4,2,128,128]{4,3,2,1,0:T(8,128)(2,1)}, u32[]{:S(2)}, u32[]{:S(2)}) async-start(bf16[16,4,2,128,128]{4,3,2,1,0:T(8,128)(2,1)} %get-tuple-element.28), calls=%async_computation | async-start | bytes 8388608 | tf_op jit(solution)/shard_map/all_to_all | solution.py:131
  218.9 91.3 %all-to-all-done = bf16[16,4,2,128,128]{4,3,2,1,0:T(8,128)(2,1)} async-done(((bf16[16,4,2,128,128]{4,3,2,1,0:T(8,128)(2,1)}), bf16[16,4,2,128,128]{4,3,2,1,0:T(8,128)(2,1)}, u32[]{:S(2)}, u32[]{:S(2)}) %all-to-all-start) | async-done | bytes 4194336 | tf_op jit(solution)/shard_map/all_to_all | solution.py:131
  310.2 7.3 %reshape.280 = bf16[64,32768]{1,0:T(8,128)(2,1)} reshape(bf16[16,4,2,128,128]{4,3,2,1,0:T(8,128)(2,1)} %all-to-all-done) | data formatting | bytes 8388608 | tf_op jit(solution)/shard_map/reshape | solution.py:143
  317.5 3.3 copy.148
  326.5 5.8 all-to-all-start.1
  332.4 48.7 %all-to-all-done.1 = f32[2,512,512]{2,0,1:T(2,128)S(1)} async-done(((f32[2,512,512]{2,0,1:T(2,128)}), f32[2,512,512]{2,0,1:T(2,128)S(1)}, u32[]{:S(2)}, u32[]{:S(2)}) %all-to-all-start.1) | async-done | bytes 2097184 | tf_op jit(solution)/shard_map/all_to_all | solution.py:150
  397.9 3.4 fusion.23
  406.1 7.9 %copy.130 = f32[2,32,8192]{1,0,2:T(2,128)} copy(f32[2,32,8192]{2,1,0:T(8,128)S(1)} %pad_maximum_fusion) | data formatting | bytes 4194304 | tf_op jit(solution)/shard_map/stack | solution.py:152
  414.0 10.3 %reshape.317 = f32[16,1,32768]{2,1,0:T(1,128)S(1)} reshape(f32[8192,2,32]{2,1,0:T(2,128)} %bitcast.179) | data formatting | bytes 4194304
  424.3 31.8 %all_to_all.53 = f32[16,1,32768]{2,1,0:T(1,128)} all-to-all(f32[16,1,32768]{2,1,0:T(1,128)S(1)} %reshape.317), channel_id=1, replica_groups=mesh['facet'=16,'span'=16] {'facet'}, dimensions={0} | all-to-all | bytes 4194304 | tf_op jit(solution)/shard_map/all_to_all | solution.py:154
  456.6 7.3 %reduce.4 = f32[16,32768]{1,0:T(8,128)S(1)} reduce(f32[16,1,32768]{2,1,0:T(1,128)} %all_to_all.53, f32[]{:T(128)} %broadcast.473), dimensions={1}, to_apply=%all_to_all.42.reduce_sub_computation | reduce | bytes 4194308 | tf_op jit(solution)/shard_map/all_to_all | solution.py:154
  463.9 9.0 %reshape.318 = f32[8192,2,32]{2,1,0:T(2,128)} reshape(f32[16,32768]{1,0:T(8,128)S(1)} %reduce.4) | data formatting | bytes 4194304
  472.9 10.2 %copy.142 = f32[2,32,16,512]{3,1,2,0:T(8,128)S(1)} copy(f32[2,32,16,512]{1,0,3,2:T(2,128)} %bitcast.180) | data formatting | bytes 4194304 | tf_op jit(solution)/shard_map/all_to_all | solution.py:154
  485.6 58.1 %all_to_all.54 = f32[2,512,512]{1,0,2:T(2,128)S(1)} all-to-all(f32[2,512,512]{1,0,2:T(2,128)} %copy.133), channel_id=1, replica_groups=mesh['facet'=16,'span'=16] {'span'}, dimensions={2} | all-to-all | bytes 4194304 | tf_op jit(solution)/shard_map/all_to_all | solution.py:153
  544.0 4.4 reshape.282
  548.5 6.1 %fusion.174 = (f32[1,32,16,16,32]{4,2,1,3,0:T(8,128)S(1)}, f32[1,32,16,16,32]{4,2,1,3,0:T(8,128)}) fusion(f32[2,32,16,16,32]{4,2,1,3,0:T(8,128)} %bitcast.181), kind=kLoop, calls=%fused_computation.251 | loop fusion | bytes 4194304 | tf_op jit(solution)/shard_map/slice | solution.py:167
  554.6 4.4 copy.135
  558.9 3.3 reshape_squeeze.14
  563.4 6.5 %copy.136 = f32[1,32,16,16,32]{4,3,2,1,0:T(8,128)} copy(f32[1,32,16,16,32]{4,2,1,3,0:T(8,128)} %get-tuple-element.70) | data formatting | bytes 2097152 | tf_op jit(solution)/shard_map/slice | solution.py:167
  569.9 3.4 reshape_squeeze.15
  (195 shorter events, 140.9 us)
Async XLA Ops:
  6.5 4.0 copy-start.1
  6.5 56.2 %all-gather.5.cloned.1.call-start = ((), (), s32[]{:S(2)}) async-start(), calls=%async_computation.5 | async-start | bytes 2228224 | tf_op jit(solution)/shard_map/all_gather | solution.py:118
  7.3 107.3 %all-gather.3.cloned.1.call-start = ((), (), s32[]{:S(2)}) async-start(), calls=%async_computation.4 | async-start | bytes 2228224 | tf_op jit(solution)/shard_map/all_gather | solution.py:117
  208.1 102.1 %all-to-all-start = ((bf16[16,4,2,128,128]{4,3,2,1,0:T(8,128)(2,1)}), bf16[16,4,2,128,128]{4,3,2,1,0:T(8,128)(2,1)}, u32[]{:S(2)}, u32[]{:S(2)}) async-start(bf16[16,4,2,128,128]{4,3,2,1,0:T(8,128)(2,1)} %get-tuple-element.28), calls=%async_computation | async-start | bytes 8388608 | tf_op jit(solution)/shard_map/all_to_all | solution.py:131
  326.5 54.6 %all-to-all-start.1 = ((f32[2,512,512]{2,0,1:T(2,128)}), f32[2,512,512]{2,0,1:T(2,128)S(1)}, u32[]{:S(2)}, u32[]{:S(2)}) async-start(f32[2,512,512]{2,0,1:T(2,128)} %reshape.314), calls=%async_computation.1 | async-start | bytes 4194304 | tf_op jit(solution)/shard_map/all_to_all | solution.py:150
  385.3 1.2 copy-start
Sparse Core Ops, SparseCore 0:
  9.8 52.8 all-gather.4
  65.2 49.3 all-gather.2
where the time goes:
time: 598 us; the launch traced here: 589 us
  waiting for transfers between devices  240 us (40%)
  local copies, waits for them, and re-layouts  133 us (22%)
  blocking collectives  89.9 us (15%)
  matrix products  72.7 us (12%)
  other arithmetic  24.1 us (4%)
  starting transfers between devices  14.4 us (2%)
  between operations  14 us (2%)
    all_to_all x1, waiting for transfers between devices, shards(): lax.all_to_all(made_subs, 'span', split_axis=0, concat_axis=0, tiled=True)  91.3 us
    all_to_all x1, blocking collectives, shards(): lax.all_to_all(lax.all_to_all(half_done, 'facet', split_axis=2, concat_ax...  58.1 us
    all_gather x1, waiting for transfers between devices, shards(): lax.all_gather(coordinates, 'facet', axis=1, tiled=True)  49.8 us
    dot_general x16, matrix products, subgrids_of(): jnp.einsum('ezkp,ekq->ezpq', weighted, col_kernel, preferred_element_type...  49.2 us
    all_gather x1, waiting for transfers between devices, shards(): lax.all_gather(rotated, 'facet', axis=1, tiled=True)  49.1 us
    all_to_all x1, waiting for transfers between devices, shards(): lax.all_to_all(block, 'span', split_axis=1, concat_axis=2, tiled=True)  48.7 us
    all_to_all x1, blocking collectives, shards(): lax.all_to_all(half_done, 'facet', split_axis=2, concat_axis=1, tiled=True)  31.8 us
    exp x16, local copies, waits for them, and re-layouts, kernel_rows(): return jnp.exp(-(gap_size * gap_size) / (2.0 * spread * spread))  29.8 us
  transfers between devices with their start and end apart: 4, of which 4 were waited for; matrix products, arithmetic and copies ran while one was open for 2% of the time, Pallas kernels for 0%

commit v1 on v0

--- a/solution.py
+++ b/solution.py
@@ -2,6 +2,7 @@
 import jax.numpy as jnp
 from jax import lax
 from jax.sharding import PartitionSpec as P
+from jax.lax import axis_index, axis_size, ppermute
 
 N = 8192
 P_SIZE = 128
@@ -86,6 +87,29 @@
 
 
 def shards(visibilities, coordinates, phases, sub_index):
+
+    def lines_finish(raw):
+        axis_name = "facet"
+        arr_now = axis_size(axis_name)
+        z, known, row_out = (arr_now, axis_index(axis_name), raw.shape[1])
+        windows = tuple((p * z if j0 == 1 else p for j0, p in enumerate(raw.shape)))
+        aux = lax.dynamic_update_slice_in_dim(
+            jnp.zeros(windows, raw.dtype), raw, known * row_out, axis=1
+        )
+        y1 = all_rows = raw
+        for s in [*range(1, z // 2 + 1)]:
+            part_now = tuple(((j0, (j0 + 1) % z) for j0 in range(z)))
+            y1 = ppermute(y1, axis_name, part_now)
+            aux = lax.dynamic_update_slice_in_dim(aux, y1, (known - s) % z * row_out, axis=1)
+            if 2 * s < z:
+                all_rows = ppermute(
+                    all_rows, axis_name, tuple(((j0, (j0 - 1) % z) for j0 in range(z)))
+                )
+                aux = lax.dynamic_update_slice_in_dim(
+                    aux, all_rows, (known + s) % z * row_out, axis=1
+                )
+        return aux
+
     facet_count = lax.axis_size("facet")
     span_count = lax.axis_size("span")
     side_count = N // P_SIZE
@@ -113,10 +137,7 @@
     flat_filled = send_filled.reshape(-1)
     entry_count = flat_ids.shape[0]
     blank = jnp.zeros((entry_count, 2, vis_count), jnp.bfloat16)
-    pieces = (
-        lax.all_gather(rotated, "facet", axis=1, tiled=True),
-        lax.all_gather(coordinates, "facet", axis=1, tiled=True),
-    )
+    pieces = (lines_finish(rotated), lax.all_gather(coordinates, "facet", axis=1, tiled=True))
     rows_here = pieces[0].shape[1]
     inside = flat_filled & (flat_ids >= 0) & (flat_ids < rows_here)
     where_row = jnp.clip(flat_ids, 0, rows_here - 1)

time: 598 us -> 576 us (0.963)
  waiting for transfers between devices: 240 us -> 169 us
  starting transfers between devices: 14.4 us -> 62 us
    all_gather x1, waiting for transfers between devices: 49.8 us -> 0.02 us  [shards(): lax.all_gather(coordinates, 'facet', axis=1, tiled=True)]
    all_gather x1 -> x0, waiting for transfers between devices: 49.1 us -> none  [shards(): lax.all_gather(rotated, 'facet', axis=1, tiled=True)]
    ppermute x0 -> x15, starting transfers between devices: none -> 36.9 us  [the longest x7 36.7 us: lines_finish(): ppermute(all_rows, axis_name, tuple(((j0, (j0 - 1) % z) for j0 in range(z...]
    ppermute x0 -> x15, waiting for transfers between devices: none -> 27.3 us  [the longest x8 17.1 us: lines_finish(): y1 = ppermute(y1, axis_name, part_now)]
    all_to_all x1, starting transfers between devices: 8.52 us -> 19.6 us  [shards(): lax.all_to_all(made_subs, 'span', split_axis=0, concat_axis=0, tiled=True)]
  transfers between devices with their start and end apart: 4 -> 18, of which waited for: 4 -> 13; matrix products, arithmetic and copies ran while one was open for 2% -> 2% of each run, Pallas kernels for 0% -> 0%
where the time goes in v1:
time: 576 us; the launch traced here: 566 us
  waiting for transfers between devices  169 us (29%)
  local copies, waits for them, and re-layouts  134 us (23%)
  blocking collectives  88.4 us (15%)
  matrix products  72.6 us (13%)
  starting transfers between devices  62 us (11%)
  other arithmetic  24.7 us (4%)
  between operations  14.7 us (3%)
    all_to_all x1, waiting for transfers between devices, shards(): lax.all_to_all(made_subs, 'span', split_axis=0, concat_axis=0, tiled=True)  93 us
    all_to_all x1, blocking collectives, shards(): lax.all_to_all(lax.all_to_all(half_done, 'facet', split_axis=2, concat_ax...  58 us
    dot_general x16, matrix products, subgrids_of(): jnp.einsum('ezkp,ekq->ezpq', weighted, col_kernel, preferred_element_type...  49.2 us
    all_to_all x1, waiting for transfers between devices, shards(): lax.all_to_all(block, 'span', split_axis=1, concat_axis=2, tiled=True)  48.8 us
    ppermute x7, starting transfers between devices, lines_finish(): ppermute(all_rows, axis_name, tuple(((j0, (j0 - 1) % z) for j0 in range(z...  36.7 us
    all_to_all x1, blocking collectives, shards(): lax.all_to_all(half_done, 'facet', split_axis=2, concat_axis=1, tiled=True)  30.4 us
    exp x16, local copies, waits for them, and re-layouts, kernel_rows(): return jnp.exp(-(gap_size * gap_size) / (2.0 * spread * spread))  29.7 us
    unnamed x7, local copies, waits for them, and re-layouts  22.7 us
  transfers between devices with their start and end apart: 18, of which 13 were waited for; matrix products, arithmetic and copies ran while one was open for 2% of the time, Pallas kernels for 0%

profile of v1, /device:TPU:1, one launch (start us, length us, event | category | flops | bytes accessed | tf_op | source)
XLA Modules:
  0.0 566.3 jit_solution(11151851214256946612)
XLA Ops:
  9.4 5.8 %collective-permute-start.1 = (bf16[1,32,2,1024]{3,2,1,0:T(2,128)(2,1)S(1)}, bf16[1,32,2,1024]{3,2,1,0:T(2,128)(2,1)S(1)}, u32[]{:S(2)}, u32[]{:S(2)}) collective-permute-start(bf16[1,32,2,1024]{3,2,1,0:T(2,128)(2,1)S(1)} %pad_maximum_fusion.1), channel_id=1, source_target_pairs={{0,240},{16,0},{32,16},{48,32},{64,48},{80,64},{96,80},{112,96},{1... | collective-permute-start | bytes 393224 | tf_op jit(solution)/shard_map/ppermute | solution.py:105
  21.6 4.9 collective-permute-start.3
  28.4 5.2 collective-permute-start.5
  35.5 5.2 collective-permute-start.7
  42.9 5.2 collective-permute-start.9
  50.1 5.2 collective-permute-start.11
  60.5 5.2 collective-permute-start.13
  66.8 7.6 %collective-permute-done.12 = bf16[1,32,2,1024]{3,2,1,0:T(2,128)(2,1)S(1)} collective-permute-done((bf16[1,32,2,1024]{3,2,1,0:T(2,128)(2,1)S(1)}, bf16[1,32,2,1024]{3,2,1,0:T(2,128)(2,1)S(1)}, u32[]{:S(2)}, u32[]{:S(2)}) %collective-permute-start.12) | collective-permute-done | bytes 131104 | tf_op jit(solution)/shard_map/ppermute | solution.py:102
  74.6 6.9 %collective-permute-done.14 = bf16[1,32,2,1024]{3,2,1,0:T(2,128)(2,1)S(1)} collective-permute-done((bf16[1,32,2,1024]{3,2,1,0:T(2,128)(2,1)S(1)}, bf16[1,32,2,1024]{3,2,1,0:T(2,128)(2,1)S(1)}, u32[]{:S(2)}, u32[]{:S(2)}) %collective-permute-start.14) | collective-permute-done | bytes 131104 | tf_op jit(solution)/shard_map/ppermute | solution.py:102
  86.1 90.1 %while.10 = (s32[]{:T(128)}, bf16[16,4,2,128,128]{4,3,2,1,0:T(8,128)(2,1)}, bf16[16,4,2,1024]{3,2,1,0:T(2,128)(2,1)S(1)}, bf16[16,4,2,1024]{3,2,1,0:T(2,128)(2,1)S(1)}, s32[]{:T(128)}) while((s32[]{:T(128)}, bf16[16,4,2,128,128]{4,3,2,1,0:T(8,128)(2,1)}, bf16[16,4,2,1024]{3,2,1,0:T(2,128)(2,1)S(1)}, bf16[16,4,2,1024]{3,2,1,0:T(2,128)(2,1)S(1)}, ...), condition=%wide.region_9.11_spmd, body=%wide.region_8.10_spmd.sunk | while | flops 275398656 | bytes 8912977 | solution.py:151
  176.2 19.6 %all-to-all-start = ((bf16[16,4,2,128,128]{4,3,2,1,0:T(8,128)(2,1)}), bf16[16,4,2,128,128]{4,3,2,1,0:T(8,128)(2,1)}, u32[]{:S(2)}, u32[]{:S(2)}) async-start(bf16[16,4,2,128,128]{4,3,2,1,0:T(8,128)(2,1)} %get-tuple-element.28), calls=%async_computation | async-start | bytes 8388608 | tf_op jit(solution)/shard_map/all_to_all | solution.py:152
  196.2 93.0 %all-to-all-done = bf16[16,4,2,128,128]{4,3,2,1,0:T(8,128)(2,1)} async-done(((bf16[16,4,2,128,128]{4,3,2,1,0:T(8,128)(2,1)}), bf16[16,4,2,128,128]{4,3,2,1,0:T(8,128)(2,1)}, u32[]{:S(2)}, u32[]{:S(2)}) %all-to-all-start) | async-done | bytes 4194336 | tf_op jit(solution)/shard_map/all_to_all | solution.py:152
  289.2 7.3 %reshape.318 = bf16[64,32768]{1,0:T(8,128)(2,1)} reshape(bf16[16,4,2,128,128]{4,3,2,1,0:T(8,128)(2,1)} %all-to-all-done) | data formatting | bytes 8388608 | tf_op jit(solution)/shard_map/reshape | solution.py:164
  305.5 5.5 all-to-all-start.1
  311.1 48.8 %all-to-all-done.1 = f32[2,512,512]{2,0,1:T(2,128)S(1)} async-done(((f32[2,512,512]{2,0,1:T(2,128)}), f32[2,512,512]{2,0,1:T(2,128)S(1)}, u32[]{:S(2)}, u32[]{:S(2)}) %all-to-all-start.1) | async-done | bytes 2097184 | tf_op jit(solution)/shard_map/all_to_all | solution.py:171
  384.9 7.9 %copy.182 = f32[2,32,8192]{1,0,2:T(2,128)} copy(f32[2,32,8192]{2,1,0:T(8,128)S(1)} %pad_maximum_fusion) | data formatting | bytes 4194304 | tf_op jit(solution)/shard_map/stack | solution.py:173
  392.9 10.3 %reshape.355 = f32[16,1,32768]{2,1,0:T(1,128)S(1)} reshape(f32[8192,2,32]{2,1,0:T(2,128)} %bitcast.200) | data formatting | bytes 4194304
  403.2 30.4 %all_to_all.53 = f32[16,1,32768]{2,1,0:T(1,128)} all-to-all(f32[16,1,32768]{2,1,0:T(1,128)S(1)} %reshape.355), channel_id=1, replica_groups=mesh['facet'=16,'span'=16] {'facet'}, dimensions={0} | all-to-all | bytes 4194304 | tf_op jit(solution)/shard_map/all_to_all | solution.py:175
  434.1 7.3 %reduce.4 = f32[16,32768]{1,0:T(8,128)S(1)} reduce(f32[16,1,32768]{2,1,0:T(1,128)} %all_to_all.53, f32[]{:T(128)} %broadcast.490), dimensions={1}, to_apply=%all_to_all.42.reduce_sub_computation | reduce | bytes 4194308 | tf_op jit(solution)/shard_map/all_to_all | solution.py:175
  441.4 9.0 %reshape.356 = f32[8192,2,32]{2,1,0:T(2,128)} reshape(f32[16,32768]{1,0:T(8,128)S(1)} %reduce.4) | data formatting | bytes 4194304
  450.4 10.2 %copy.194 = f32[2,32,16,512]{3,1,2,0:T(8,128)S(1)} copy(f32[2,32,16,512]{1,0,3,2:T(2,128)} %bitcast.201) | data formatting | bytes 4194304 | tf_op jit(solution)/shard_map/all_to_all | solution.py:175
  463.0 58.0 %all_to_all.54 = f32[2,512,512]{1,0,2:T(2,128)S(1)} all-to-all(f32[2,512,512]{1,0,2:T(2,128)} %copy.185), channel_id=1, replica_groups=mesh['facet'=16,'span'=16] {'span'}, dimensions={2} | all-to-all | bytes 4194304 | tf_op jit(solution)/shard_map/all_to_all | solution.py:174
  525.8 6.1 %fusion.172 = (f32[1,32,16,16,32]{4,2,1,3,0:T(8,128)S(1)}, f32[1,32,16,16,32]{4,2,1,3,0:T(8,128)}) fusion(f32[2,32,16,16,32]{4,2,1,3,0:T(8,128)} %bitcast.202), kind=kLoop, calls=%fused_computation.266 | loop fusion | bytes 4194304 | tf_op jit(solution)/shard_map/slice | solution.py:188
  540.7 6.6 %copy.188 = f32[1,32,16,16,32]{4,3,2,1,0:T(8,128)} copy(f32[1,32,16,16,32]{4,2,1,3,0:T(8,128)} %get-tuple-element.78) | data formatting | bytes 2097152 | tf_op jit(solution)/shard_map/slice | solution.py:188
  (241 shorter events, 179.8 us)
Async XLA Ops:
  6.5 8.8 %copy-start.1 = (s32[16,512]{1,0:T(8,128)S(1)}, s32[16,512]{1,0:T(8,128)}, u32[]{:S(2)}) copy-start(s32[16,512]{1,0:T(8,128)} %param.11) | copy-start | bytes 98308
  6.5 76.2 %all-gather.2.cloned.1.call-start = ((), (), s32[]{:S(2)}) async-start(), calls=%async_computation.4 | async-start | bytes 2228224 | tf_op jit(solution)/shard_map/all_gather | solution.py:140
  9.4 12.2 %collective-permute-start.1 = (bf16[1,32,2,1024]{3,2,1,0:T(2,128)(2,1)S(1)}, bf16[1,32,2,1024]{3,2,1,0:T(2,128)(2,1)S(1)}, u32[]{:S(2)}, u32[]{:S(2)}) collective-permute-start(bf16[1,32,2,1024]{3,2,1,0:T(2,128)(2,1)S(1)} %pad_maximum_fusion.1), channel_id=1, source_target_pairs={{0,240},{16,0},{32,16},{48,32},{64,48},{80,64},{96,80},{112,96},{1... | collective-permute-start | bytes 393224 | tf_op jit(solution)/shard_map/ppermute | solution.py:105
  15.3 11.2 %collective-permute-start = (bf16[1,32,2,1024]{3,2,1,0:T(2,128)(2,1)S(1)}, bf16[1,32,2,1024]{3,2,1,0:T(2,128)(2,1)S(1)}, u32[]{:S(2)}, u32[]{:S(2)}) collective-permute-start(bf16[1,32,2,1024]{3,2,1,0:T(2,128)(2,1)S(1)} %pad_maximum_fusion.1), channel_id=1, source_target_pairs={{0,16},{16,32},{32,48},{48,64},{64,80},{80,96},{96,112},{112,128},... | collective-permute-start | bytes 393224 | tf_op jit(solution)/shard_map/ppermute | solution.py:102
  21.6 6.8 %collective-permute-start.3 = (bf16[1,32,2,1024]{3,2,1,0:T(2,128)(2,1)S(1)}, bf16[1,32,2,1024]{3,2,1,0:T(2,128)(2,1)S(1)}, u32[]{:S(2)}, u32[]{:S(2)}) collective-permute-start(bf16[1,32,2,1024]{3,2,1,0:T(2,128)(2,1)S(1)} %collective-permute-done.1), channel_id=1, source_target_pairs={{0,240},{16,0},{32,16},{48,32},{64,48},{80,64},{96,80},{112,96},{1... | collective-permute-start | bytes 393224 | tf_op jit(solution)/shard_map/ppermute | solution.py:105
  26.5 7.1 %collective-permute-start.2 = (bf16[1,32,2,1024]{3,2,1,0:T(2,128)(2,1)S(1)}, bf16[1,32,2,1024]{3,2,1,0:T(2,128)(2,1)S(1)}, u32[]{:S(2)}, u32[]{:S(2)}) collective-permute-start(bf16[1,32,2,1024]{3,2,1,0:T(2,128)(2,1)S(1)} %collective-permute-done), channel_id=1, source_target_pairs={{0,16},{16,32},{32,48},{48,64},{64,80},{80,96},{96,112},{112,128},... | collective-permute-start | bytes 393224 | tf_op jit(solution)/shard_map/ppermute | solution.py:102
  28.4 7.1 %collective-permute-start.5 = (bf16[1,32,2,1024]{3,2,1,0:T(2,128)(2,1)S(1)}, bf16[1,32,2,1024]{3,2,1,0:T(2,128)(2,1)S(1)}, u32[]{:S(2)}, u32[]{:S(2)}) collective-permute-start(bf16[1,32,2,1024]{3,2,1,0:T(2,128)(2,1)S(1)} %collective-permute-done.3), channel_id=1, source_target_pairs={{0,240},{16,0},{32,16},{48,32},{64,48},{80,64},{96,80},{112,96},{1... | collective-permute-start | bytes 393224 | tf_op jit(solution)/shard_map/ppermute | solution.py:105
  33.6 7.8 %collective-permute-start.4 = (bf16[1,32,2,1024]{3,2,1,0:T(2,128)(2,1)S(1)}, bf16[1,32,2,1024]{3,2,1,0:T(2,128)(2,1)S(1)}, u32[]{:S(2)}, u32[]{:S(2)}) collective-permute-start(bf16[1,32,2,1024]{3,2,1,0:T(2,128)(2,1)S(1)} %collective-permute-done.2), channel_id=1, source_target_pairs={{0,16},{16,32},{32,48},{48,64},{64,80},{80,96},{96,112},{112,128},... | collective-permute-start | bytes 393224 | tf_op jit(solution)/shard_map/ppermute | solution.py:102
  35.5 7.4 %collective-permute-start.7 = (bf16[1,32,2,1024]{3,2,1,0:T(2,128)(2,1)S(1)}, bf16[1,32,2,1024]{3,2,1,0:T(2,128)(2,1)S(1)}, u32[]{:S(2)}, u32[]{:S(2)}) collective-permute-start(bf16[1,32,2,1024]{3,2,1,0:T(2,128)(2,1)S(1)} %collective-permute-done.5), channel_id=1, source_target_pairs={{0,240},{16,0},{32,16},{48,32},{64,48},{80,64},{96,80},{112,96},{1... | collective-permute-start | bytes 393224 | tf_op jit(solution)/shard_map/ppermute | solution.py:105
  41.4 7.1 %collective-permute-start.6 = (bf16[1,32,2,1024]{3,2,1,0:T(2,128)(2,1)S(1)}, bf16[1,32,2,1024]{3,2,1,0:T(2,128)(2,1)S(1)}, u32[]{:S(2)}, u32[]{:S(2)}) collective-permute-start(bf16[1,32,2,1024]{3,2,1,0:T(2,128)(2,1)S(1)} %collective-permute-done.4), channel_id=1, source_target_pairs={{0,16},{16,32},{32,48},{48,64},{64,80},{80,96},{96,112},{112,128},... | collective-permute-start | bytes 393224 | tf_op jit(solution)/shard_map/ppermute | solution.py:102
  42.9 7.2 %collective-permute-start.9 = (bf16[1,32,2,1024]{3,2,1,0:T(2,128)(2,1)S(1)}, bf16[1,32,2,1024]{3,2,1,0:T(2,128)(2,1)S(1)}, u32[]{:S(2)}, u32[]{:S(2)}) collective-permute-start(bf16[1,32,2,1024]{3,2,1,0:T(2,128)(2,1)S(1)} %collective-permute-done.7), channel_id=1, source_target_pairs={{0,240},{16,0},{32,16},{48,32},{64,48},{80,64},{96,80},{112,96},{1... | collective-permute-start | bytes 393224 | tf_op jit(solution)/shard_map/ppermute | solution.py:105
  48.6 7.3 %collective-permute-start.8 = (bf16[1,32,2,1024]{3,2,1,0:T(2,128)(2,1)S(1)}, bf16[1,32,2,1024]{3,2,1,0:T(2,128)(2,1)S(1)}, u32[]{:S(2)}, u32[]{:S(2)}) collective-permute-start(bf16[1,32,2,1024]{3,2,1,0:T(2,128)(2,1)S(1)} %collective-permute-done.6), channel_id=1, source_target_pairs={{0,16},{16,32},{32,48},{48,64},{64,80},{80,96},{96,112},{112,128},... | collective-permute-start | bytes 393224 | tf_op jit(solution)/shard_map/ppermute | solution.py:102
  50.1 10.4 %collective-permute-start.11 = (bf16[1,32,2,1024]{3,2,1,0:T(2,128)(2,1)S(1)}, bf16[1,32,2,1024]{3,2,1,0:T(2,128)(2,1)S(1)}, u32[]{:S(2)}, u32[]{:S(2)}) collective-permute-start(bf16[1,32,2,1024]{3,2,1,0:T(2,128)(2,1)S(1)} %collective-permute-done.9), channel_id=1, source_target_pairs={{0,240},{16,0},{32,16},{48,32},{64,48},{80,64},{96,80},{112,96},{1... | collective-permute-start | bytes 393224 | tf_op jit(solution)/shard_map/ppermute | solution.py:105
  55.9 10.6 %collective-permute-start.10 = (bf16[1,32,2,1024]{3,2,1,0:T(2,128)(2,1)S(1)}, bf16[1,32,2,1024]{3,2,1,0:T(2,128)(2,1)S(1)}, u32[]{:S(2)}, u32[]{:S(2)}) collective-permute-start(bf16[1,32,2,1024]{3,2,1,0:T(2,128)(2,1)S(1)} %collective-permute-done.8), channel_id=1, source_target_pairs={{0,16},{16,32},{32,48},{48,64},{64,80},{80,96},{96,112},{112,128},... | collective-permute-start | bytes 393224 | tf_op jit(solution)/shard_map/ppermute | solution.py:102
  60.5 14.0 %collective-permute-start.13 = (bf16[1,32,2,1024]{3,2,1,0:T(2,128)(2,1)S(1)}, bf16[1,32,2,1024]{3,2,1,0:T(2,128)(2,1)S(1)}, u32[]{:S(2)}, u32[]{:S(2)}) collective-permute-start(bf16[1,32,2,1024]{3,2,1,0:T(2,128)(2,1)S(1)} %collective-permute-done.11), channel_id=1, source_target_pairs={{0,240},{16,0},{32,16},{48,32},{64,48},{80,64},{96,80},{112,96},{1... | collective-permute-start | bytes 393224 | tf_op jit(solution)/shard_map/ppermute | solution.py:105
  66.5 7.8 %collective-permute-start.12 = (bf16[1,32,2,1024]{3,2,1,0:T(2,128)(2,1)S(1)}, bf16[1,32,2,1024]{3,2,1,0:T(2,128)(2,1)S(1)}, u32[]{:S(2)}, u32[]{:S(2)}) collective-permute-start(bf16[1,32,2,1024]{3,2,1,0:T(2,128)(2,1)S(1)} %collective-permute-done.10), channel_id=1, source_target_pairs={{0,16},{16,32},{32,48},{48,64},{64,80},{80,96},{96,112},{112,128},... | collective-permute-start | bytes 393224 | tf_op jit(solution)/shard_map/ppermute | solution.py:102
  74.4 7.1 %collective-permute-start.14 = (bf16[1,32,2,1024]{3,2,1,0:T(2,128)(2,1)S(1)}, bf16[1,32,2,1024]{3,2,1,0:T(2,128)(2,1)S(1)}, u32[]{:S(2)}, u32[]{:S(2)}) collective-permute-start(bf16[1,32,2,1024]{3,2,1,0:T(2,128)(2,1)S(1)} %collective-permute-done.12), channel_id=1, source_target_pairs={{0,16},{16,32},{32,48},{48,64},{64,80},{80,96},{96,112},{112,128},... | collective-permute-start | bytes 393224 | tf_op jit(solution)/shard_map/ppermute | solution.py:102
  176.2 113.0 %all-to-all-start = ((bf16[16,4,2,128,128]{4,3,2,1,0:T(8,128)(2,1)}), bf16[16,4,2,128,128]{4,3,2,1,0:T(8,128)(2,1)}, u32[]{:S(2)}, u32[]{:S(2)}) async-start(bf16[16,4,2,128,128]{4,3,2,1,0:T(8,128)(2,1)} %get-tuple-element.28), calls=%async_computation | async-start | bytes 8388608 | tf_op jit(solution)/shard_map/all_to_all | solution.py:152
  305.5 54.5 %all-to-all-start.1 = ((f32[2,512,512]{2,0,1:T(2,128)}), f32[2,512,512]{2,0,1:T(2,128)S(1)}, u32[]{:S(2)}, u32[]{:S(2)}) async-start(f32[2,512,512]{2,0,1:T(2,128)} %reshape.352), calls=%async_computation.1 | async-start | bytes 4194304 | tf_op jit(solution)/shard_map/all_to_all | solution.py:171
  364.1 1.2 copy-start
Sparse Core Ops, SparseCore 0:
  15.4 55.3 all-gather.1
